TPU v7x, 256 devices: a whole 4x4x8 slice. The times are simulated.
256 devices in a mesh: src: 16 (over x_lo, y, core), rcv: 16 (over z, x_hi).
Axes of the slice: x: 4 (x_hi: 2, x_lo: 2; x = x_hi * 2 + x_lo), y: 4, z: 8, core: 2. Of those that a mesh axis runs over, the one named last changes fastest.
Arguments:
- recorded: bfloat16 [2, 16384, 16384], P(None, 'src', 'rcv'), may hold values from -6 to 6
- obliquity: float32 [16, 1024], replicated, may hold values from 0.01 to 0.25
- clip_level: float32 [16384], P('src'), may hold values from 0.3 to 3
Outputs:
- first_pass: bfloat16 [2, 16384, 16384], P(None, 'src', 'rcv')
- primaries: bfloat16 [2, 16384, 16384], P(None, 'src', 'rcv')
All inputs are finite; a program needn't handle non-finite values.
Results may differ from a plain program's by a relative error of at most 0.0025.
Values may be sent and summed in bfloat16 or wider, within the bound.
A program may use at most 128 MiB of HBM per device.

v0:
```python
import math

import jax
import jax.numpy as jnp
from jax import lax
from jax.sharding import PartitionSpec as P

N = 16384
K = 256


TWO_PI = 2.0 * math.pi


def rotate(real_part, imag_part, cosine, sine_part):
    return (real_part * cosine - imag_part * sine_part, real_part * sine_part + imag_part * cosine)


def twiddle(real_part, imag_part, column_index, group_index, orient, total_length):
    angles = (column_index * group_index % total_length).astype(jnp.float32) * (
        TWO_PI / total_length
    )
    return rotate(real_part, imag_part, jnp.cos(angles), orient * jnp.sin(angles))


def long_table(length, orient):
    index_left = lax.broadcasted_iota(jnp.int32, (length, length), 0)
    index_right = lax.broadcasted_iota(jnp.int32, (length, length), 1)
    angles = (index_left * index_right % length).astype(jnp.float32) * (TWO_PI / length)
    cosine = jnp.cos(angles)
    sine_part = orient * jnp.sin(angles)
    upper = jnp.concatenate([cosine, sine_part], axis=1)
    lower = jnp.concatenate([-sine_part, cosine], axis=1)
    return jnp.concatenate([upper, lower], axis=0)


def long_transform(real_part, imag_part, orient):
    length = real_part.shape[-1]
    joined = jnp.concatenate([real_part, imag_part], axis=-1)
    result = jnp.dot(
        joined.reshape(-1, 2 * length),
        long_table(length, orient),
        precision=lax.Precision.HIGHEST,
        preferred_element_type=jnp.float32,
    )
    result = result.reshape(joined.shape)
    return (result[..., :length], result[..., length:])


def across_groups(real_part, imag_part, groups, orient):
    index_left = lax.broadcasted_iota(jnp.int32, (groups, groups), 0)
    index_right = lax.broadcasted_iota(jnp.int32, (groups, groups), 1)
    angles = (index_left * index_right % groups).astype(jnp.float32) * (TWO_PI / groups)
    cosine = jnp.cos(angles)
    sine_part = orient * jnp.sin(angles)
    highest = lax.Precision.HIGHEST
    new_real = jnp.einsum("mgc,gk->mkc", real_part, cosine, precision=highest) - jnp.einsum(
        "mgc,gk->mkc", imag_part, sine_part, precision=highest
    )
    new_imag = jnp.einsum("mgc,gk->mkc", real_part, sine_part, precision=highest) + jnp.einsum(
        "mgc,gk->mkc", imag_part, cosine, precision=highest
    )
    return (new_real, new_imag)


def filter_rows(whole_rows, obliquity, groups):
    row_total = whole_rows.shape[1]
    group_cols = whole_rows.shape[2] // groups
    total_length = groups * group_cols
    values = whole_rows.astype(jnp.float32).reshape(2, row_total, groups, group_cols)
    real_part, imag_part = across_groups(values[0], values[1], groups, -1.0)
    column_index = lax.broadcasted_iota(jnp.int32, (1, 1, group_cols), 2)
    group_index = lax.broadcasted_iota(jnp.int32, (1, groups, 1), 1)
    real_part, imag_part = twiddle(
        real_part, imag_part, column_index, group_index, -1.0, total_length
    )
    real_part, imag_part = long_transform(real_part, imag_part, -1.0)
    real_part = real_part * obliquity[None]
    imag_part = imag_part * obliquity[None]
    real_part, imag_part = long_transform(real_part, imag_part, 1.0)
    real_part, imag_part = twiddle(
        real_part, imag_part, column_index, group_index, 1.0, total_length
    )
    real_part, imag_part = across_groups(real_part, imag_part, groups, 1.0)
    inverse_scale = 1.0 / total_length
    returned = jnp.stack([real_part * inverse_scale, imag_part * inverse_scale])
    return returned.reshape(2, row_total, total_length).astype(jnp.bfloat16)


def through_rows(panel_rows, obliquity):
    moved_rows = lax.all_to_all(panel_rows, "rcv", split_axis=1, concat_axis=2, tiled=True)
    returned = filter_rows(moved_rows, obliquity, lax.axis_size("rcv"))
    return lax.all_to_all(returned, "rcv", split_axis=2, concat_axis=1, tiled=True)


def complex_product(left_rows, right_rows):
    left_joined = jnp.concatenate([left_rows[0], left_rows[1]], axis=0)
    upper = jnp.concatenate([right_rows[0], right_rows[1]], axis=1)
    lower = jnp.concatenate([-right_rows[1], right_rows[0]], axis=1)
    right_joined = jnp.concatenate([upper, lower], axis=0)
    return lax.dot_general(
        left_joined, right_joined, (((0,), (0,)), ((), ())), preferred_element_type=jnp.float32
    )


def per_device(recorded, obliquity, clip_level):
    spacing = N // K
    row_total = recorded.shape[1]
    col_total = recorded.shape[2]
    panel_rows = recorded.reshape(2, row_total // spacing, spacing, col_total)[:, :, 0, :]
    filtered = through_rows(panel_rows, obliquity)
    clip_rows = clip_level[:, None]
    estimate = recorded
    passes = []
    for update_index in range(2):
        columns = estimate.reshape(2, row_total, col_total // spacing, spacing)[:, :, :, 0]
        left_local = jnp.swapaxes(columns, 1, 2)
        left_panel = lax.all_gather(left_local, "rcv", axis=1, tiled=True)

        def accumulate(running, panel_piece, first_row, left_all=left_panel):
            return complex_product(left_all, panel_piece)

        zeros_init = jnp.zeros((row_total, 2 * col_total), jnp.float32)
        product_sum = accumulate(
            zeros_init, lax.all_gather(filtered, "src", axis=1, tiled=True), jnp.int32(0)
        )
        pred_real = product_sum[:, :col_total]
        pred_imag = product_sum[:, col_total:]
        limiter = lax.rsqrt(
            1.0 + (pred_real * pred_real + pred_imag * pred_imag) / (clip_rows * clip_rows)
        )
        estimate = (
            recorded.astype(jnp.float32) - jnp.stack([pred_real * limiter, pred_imag * limiter])
        ).astype(jnp.bfloat16)
        passes.append(estimate)
    return (passes[0], passes[1])


def solution(mesh):
    return jax.shard_map(
        per_device,
        mesh=mesh,
        in_specs=(P(None, "src", "rcv"), P(), P("src")),
        out_specs=(P(None, "src", "rcv"), P(None, "src", "rcv")),
        check_vma=False,
    )
```

profile of v0, /device:TPU:1, one launch (start us, length us, event | category | flops | bytes accessed | tf_op | source)
XLA Modules:
  0.0 443.9 jit_solution(7777668069207956827)
XLA Ops:
  7.2 1.1 slice.88
  8.3 0.7 copy.65
  9.0 11.6 %all-to-all-start = ((bf16[2,16,1024]{2,0,1:T(2,128)(2,1)}), bf16[2,16,1024]{2,0,1:T(2,128)(2,1)S(1)}, u32[]{:S(2)}, u32[]{:S(2)}) async-start(bf16[2,16,1024]{2,0,1:T(2,128)(2,1)} %bitcast.83), calls=%async_computation | async-start | bytes 131072 | tf_op jit(solution)/shard_map/all_to_all | solution.py:91
  20.6 0.0 all-gather.4.cloned.1.call-start
  20.6 6.2 %copy.36 = bf16[2,1024,1024]{1,2,0:T(8,128)(2,1)} copy(bf16[2,1024,1024]{2,1,0:T(8,128)(2,1)} %param.3) | data formatting | bytes 8388608 | tf_op args[0]
  26.8 1.1 slice.85
  28.0 0.7 copy.64
  28.6 0.0 all-gather.4.cloned.1.call-update
  28.6 0.0 all-gather.6.cloned.1.call-start
  28.7 17.6 %broadcast_multiply_fusion = (f32[1024,1024]{1,0:T(8,128)}, f32[1024,1024]{1,0:T(8,128)}) fusion(), kind=kLoop, calls=%fused_computation.35 | loop fusion | flops 15728640 | bytes 8388608 | tf_op jit(solution)/shard_map/mul | solution.py:31
  46.3 16.3 %fusion.27 = f32[1024,1024]{1,0:T(8,128)} fusion(), kind=kLoop, calls=%fused_computation.39 | loop fusion | flops 16777216 | bytes 4194304 | tf_op jit(solution)/shard_map/neg | solution.py:33
  62.7 16.8 %fusion.24 = (f32[1024,1024]{1,0:T(8,128)}, f32[1024,1024]{1,0:T(8,128)}) fusion(), kind=kLoop, calls=%fused_computation.36 | loop fusion | flops 15728640 | bytes 8388608 | tf_op jit(solution)/shard_map/sin | solution.py:31
  79.5 0.0 all-to-all-done
  79.5 0.1 fusion.138
  79.6 0.3 fusion.65
  79.9 0.3 fusion.66
  80.2 0.3 convolution_add_fusion.1
  80.5 0.5 subtract_bitcast_fusion
  80.9 0.0 copy-start.2
  80.9 13.8 %fusion.21 = f32[1,16,2048]{2,1,0:T(8,128)S(1)} fusion(f32[1024,1024]{1,0:T(8,128)} %get-tuple-element.19, f32[1024,1024]{1,0:T(8,128)} %fusion.27, f32[1024,1024]{1,0:T(8,128)} %get-tuple-element.18, f32[1,16,1024]{2,1,0:T(8,128)S(1)} %get-tuple-element.15, f32[1,16,1024]{2,1,0:T(8,128)S(1)} %get-tuple-element.14), kind=kOutput, calls=%fused_computation.33 | convolution fusion | flops 817922048 | bytes 12845056 | tf_op jit(solution)/shard_map/dot_general | solution.py:40
  94.8 0.0 copy-done.2
  94.8 14.4 %fusion.18 = f32[1,16,2048]{2,1,0:T(8,128)S(1)} fusion(f32[1024,1024]{1,0:T(8,128)} %get-tuple-element.19, f32[1024,1024]{1,0:T(8,128)} %get-tuple-element.21, f32[1024,1024]{1,0:T(8,128)} %get-tuple-element.20, f32[1,16,1024]{2,1,0:T(8,128)S(1)} %get-tuple-element.13, f32[1,16,1024]{2,1,0:T(8,128)S(1)} %get-tuple-element.12), kind=kOutput, calls=%fused_computation.32 | convolution fusion | flops 817922048 | bytes 12845056 | tf_op jit(solution)/shard_map/dot_general | solution.py:40
  109.2 0.5 fusion.54
  109.7 0.5 fusion.30
  110.2 0.5 fusion.52
  110.7 11.5 %stack.36 = bf16[1,1,16384]{0,1,2:T(2,128)(2,1)} reshape(bf16[16,1024]{1,0:T(8,128)(2,1)S(1)} %fusion.30) | data formatting | bytes 65536 | tf_op jit(solution)/shard_map/stack | solution.py:86
  122.2 0.5 fusion.31
  122.7 11.7 %stack.37 = bf16[1,1,16384]{0,1,2:T(2,128)(2,1)} reshape(bf16[16,1024]{1,0:T(8,128)(2,1)S(1)} %fusion.31) | data formatting | bytes 65536 | tf_op jit(solution)/shard_map/stack | solution.py:86
  134.4 25.2 %fusion.139 = bf16[16384,1,2]{2,1,0:T(2,128)(2,1)} fusion(bf16[1,1,16384]{0,1,2:T(2,128)(2,1)} %stack.37, bf16[1,1,16384]{0,1,2:T(2,128)(2,1)} %stack.36), kind=kLoop, calls=%fused_computation.177 | loop fusion | flops 131072 | bytes 131072
  159.6 0.5 broadcast.277
  160.1 90.8 %reduce = bf16[16384,2]{1,0:T(8,128)(2,1)} reduce(bf16[16384,1,2]{2,1,0:T(2,128)(2,1)} %fusion.139, bf16[]{:T(256)} %broadcast.277), dimensions={1}, to_apply=%fusion.139.reduce_sub_computation | reduce | bytes 131074
  250.9 7.2 %reshape.220 = bf16[16,2,1024]{2,1,0:T(2,128)(2,1)S(1)} reshape(bf16[16384,2]{1,0:T(8,128)(2,1)} %reduce) | data formatting | bytes 131072
  258.1 18.3 %all_to_all.21 = bf16[16,2,1024]{2,1,0:T(2,128)(2,1)S(1)} all-to-all(bf16[16,2,1024]{2,1,0:T(2,128)(2,1)S(1)} %reshape.220), channel_id=1, replica_groups=mesh['src'=16,'rcv'=16] {'rcv'}, dimensions={0} | all-to-all | bytes 131072 | tf_op jit(solution)/shard_map/all_to_all | solution.py:93
  276.4 11.9 %reshape.221 = bf16[16384,1,2]{2,1,0:T(2,128)(2,1)} reshape(bf16[16,2,1024]{2,1,0:T(2,128)(2,1)S(1)} %all_to_all.21) | data formatting | bytes 131072
  288.3 0.0 copy-start.3
  288.3 15.4 %copy.42 = bf16[2,1,16384]{2,0,1:T(2,128)(2,1)S(1)} copy(bf16[2,1,16384]{0,1,2:T(2,128)(2,1)} %bitcast.85) | data formatting | bytes 131072 | tf_op jit(solution)/shard_map/all_to_all | solution.py:93
  303.7 0.7 copy.62
  304.3 0.0 all-gather.6.cloned.1.call-update
  304.3 0.3 all-gather.8.cloned.1.call-start
  304.6 0.0 copy-done.3
  304.6 0.0 all-gather.4.cloned.1.call-done
  304.7 1.3 slice_bitcast_fusion.5
  305.9 29.6 %all-gather.6.cloned.1.call-done = bf16[2,256,1024]{2,1,0:T(8,128)(2,1)} async-done(((bf16[2,16,1024]{2,1,0:T(8,128)(2,1)}), bf16[2,256,1024]{2,1,0:T(8,128)(2,1)}) %all-gather.6.cloned.1.call-update) | async-done | bytes 1048592 | tf_op jit(solution)/shard_map/all_gather | solution.py:125
  335.6 1.3 slice_bitcast_fusion.2
  336.8 1.1 fusion.137
  337.9 2.4 fusion.32
  340.3 0.0 copy-start
  340.3 2.4 multiply_bitcast_fusion.3
  342.8 0.0 copy-done
  342.8 3.0 fusion.10
  345.8 6.2 %copy.43 = bf16[2,1024,1024]{1,2,0:T(8,128)(2,1)} copy(bf16[2,1024,1024]{2,1,0:T(8,128)(2,1)} %fusion.10) | data formatting | bytes 8388608 | tf_op jit(solution)/shard_map/convert_element_type | solution.py:134
  352.0 1.1 slice.99
  353.1 0.7 copy.63
  353.8 0.0 all-gather.8.cloned.1.call-update
  353.8 74.2 %all-gather.8.cloned.1.call-done = bf16[2,256,1024]{2,1,0:T(8,128)(2,1)} async-done(((bf16[2,16,1024]{2,1,0:T(8,128)(2,1)}), bf16[2,256,1024]{2,1,0:T(8,128)(2,1)}) %all-gather.8.cloned.1.call-update) | async-done | bytes 1048592 | tf_op jit(solution)/shard_map/all_gather | solution.py:118
  428.0 1.3 slice_bitcast_fusion.1
  429.2 2.4 fusion.36
  431.6 0.0 copy-start.1
  431.7 2.4 multiply_bitcast_fusion.1
  434.1 0.0 copy-done.1
  434.1 3.0 fusion.11
  (2 shorter events, 0.0 us)
Async XLA Ops:
  9.0 70.5 %all-to-all-start = ((bf16[2,16,1024]{2,0,1:T(2,128)(2,1)}), bf16[2,16,1024]{2,0,1:T(2,128)(2,1)S(1)}, u32[]{:S(2)}, u32[]{:S(2)}) async-start(bf16[2,16,1024]{2,0,1:T(2,128)(2,1)} %bitcast.83), calls=%async_computation | async-start | bytes 131072 | tf_op jit(solution)/shard_map/all_to_all | solution.py:91
  20.6 284.1 %all-gather.4.cloned.1.call-start = ((), (), s32[]{:S(2)}) async-start(), calls=%async_computation.2 | async-start | bytes 1114112 | tf_op jit(solution)/shard_map/all_gather | solution.py:118
  28.6 306.9 %all-gather.6.cloned.1.call-start = ((), (), s32[]{:S(2)}) async-start(), calls=%async_computation.3 | async-start | bytes 1114112 | tf_op jit(solution)/shard_map/all_gather | solution.py:125
  80.9 13.9 %copy-start.2 = (f32[16,1024]{1,0:T(8,128)S(1)}, f32[16,1024]{1,0:T(8,128)}, u32[]{:S(2)}) copy-start(f32[16,1024]{1,0:T(8,128)} %param.4) | copy-start | bytes 196612
  288.3 16.3 %copy-start.3 = (f32[1024]{0:T(1024)S(1)}, f32[1024]{0:T(1024)}, u32[]{:S(2)}) copy-start(f32[1024]{0:T(1024)} %param.5) | copy-start | bytes 12292
  304.3 123.6 %all-gather.8.cloned.1.call-start = ((), (), s32[]{:S(2)}) async-start(), calls=%async_computation.4 | async-start | bytes 1114112 | tf_op jit(solution)/shard_map/all_gather | solution.py:118
  340.3 2.5 copy-start
  431.6 2.5 copy-start.1
Sparse Core Ops, SparseCore 0:
  28.8 76.2 all-gather.3
  304.5 31.0 all-gather.5
  353.9 74.0 all-gather.7
where the time goes:
time: 452 us; the launch traced here: 444 us
  other arithmetic  179 us (40%)
  waiting for transfers between devices  104 us (23%)
  local copies, waits for them, and re-layouts  80.5 us (18%)
  matrix products  36.3 us (8%)
  blocking collectives  18.3 us (4%)
  between operations  14.2 us (3%)
  starting transfers between devices  11.9 us (3%)
    unnamed x2, other arithmetic  116 us
    all_gather x2, waiting for transfers between devices, per_device(): left_panel = lax.all_gather(left_local, 'rcv', axis=1, tiled=True)  74.2 us
    all_gather x1, waiting for transfers between devices, per_device(): lax.all_gather(filtered, 'src', axis=1, tiled=True)  29.6 us
    dot_general x2, matrix products, long_transform(): jnp.dot(joined.reshape(-1, 2 * length), long_table(length, orient), preci...  28.2 us
    unnamed x15, local copies, waits for them, and re-layouts  27.8 us
    another operation x2, local copies, waits for them, and re-layouts, filter_rows(): returned = jnp.stack([real_part * inverse_scale, imag_part * inverse_scale])  23.2 us
    all_to_all x1, blocking collectives, through_rows(): lax.all_to_all(returned, 'rcv', split_axis=2, concat_axis=1, tiled=True)  18.3 us
    mul x1, other arithmetic, long_table(): sine_part = orient * jnp.sin(angles)  17.6 us
  transfers between devices with their start and end apart: 4, of which 2 were waited for; matrix products, arithmetic and copies ran while one was open for 60% of the time, Pallas kernels for 0%

commit v1 on v0

v1 whole, which is shorter than its diff:
```python
import functools

import jax
import jax.numpy as jnp
import numpy as np
from jax import lax
from jax.experimental import pallas as pl
from jax.experimental.pallas import tpu as pltpu
from jax.sharding import PartitionSpec as P

N = 16384
K = 256
MESH = pl.DeviceIdType.MESH
F32 = jnp.float32
BF16 = jnp.bfloat16
HIGHEST = lax.Precision.HIGHEST
NR = 16
NS = 16
ROWS = 1024
COLS = 1024
WIDE = COLS + K


def tables():
    k1 = np.arange(128)
    rho = np.arange(256)
    n1 = 8 * ((rho >> 1) & 15) + (rho >> 5)
    part = rho & 1
    theta = 2 * np.pi * ((k1[:, None] * n1[None, :]) % 128) / 128
    cos, sin = np.cos(theta), np.sin(theta)
    even = part[None, :] == 0
    m1 = np.concatenate([np.where(even, cos, sin), np.where(even, -sin, cos)], axis=0)
    m4 = np.concatenate([np.where(even, cos, sin).T, np.where(even, -sin, cos).T], axis=1)
    angle = 2 * np.pi * ((k1[:, None] * k1[None, :]) % 128) / 128
    cos, sin = np.cos(angle), np.sin(angle)
    m2 = np.block([[cos, -sin], [sin, cos]])
    m3 = np.block([[cos, sin], [-sin, cos]])
    phi = 2 * np.pi * (k1[:, None] * k1[None, :]) / N
    twiddle = np.stack([np.cos(phi), np.sin(phi)])
    return np.stack([m1, m2, m3, m4]).astype(np.float32), twiddle.astype(np.float32)


def gather_kernel(
    rec_hbm, obl_ref, dft_ref, twi_ref, left_hbm, filt_hbm,
    rec, send1, recv1, send2, recv2, lbuf, fbuf, lnat, weights,
    rec_sem, out_sem, s1_sem, r1_sem, s2_sem, r2_sem, ls_sem, lr_sem, fs_sem, fr_sem,
):
    s = lax.axis_index("src")
    r = lax.axis_index("rcv")
    z, xh = r // 2, lax.rem(r, 2)
    xl, y, c = s // 8, lax.rem(s // 2, 4), lax.rem(s, 2)

    def src_of(x, yy, core):
        return x * 8 + lax.rem(yy + 8, 4) * 2 + core

    def rcv_of(zz, x):
        return lax.rem(zz + 16, 8) * 2 + x

    def to_rcv(index):
        return (s, index)

    def to_src(index):
        return (index, r)

    peers = [to_rcv(lax.rem(r + d, NR)) for d in range(1, NR)]
    x_peer = src_of(1 - xl, y, c)
    up, down = src_of(xl, y + 1, c), src_of(xl, y - 1, c)
    mate = src_of(xl, y, 1 - c)
    peers += [to_src(i) for i in (x_peer, up, down, mate)]

    barrier = pltpu.get_barrier_semaphore()
    for peer in peers:
        pl.semaphore_signal(barrier, inc=1, device_id=peer, device_id_type=MESH)

    chunk = ROWS // 4
    loads = []
    for q in range(4):
        load = pltpu.make_async_copy(
            rec_hbm.at[:, pl.ds(q * chunk, chunk), :], rec.at[:, pl.ds(q * chunk, chunk), :], rec_sem.at[q]
        )
        load.start()
        loads.append(load)

    obl = obl_ref[...] * (1.0 / N)
    hi = obl.astype(BF16)
    rest = obl - hi.astype(F32)
    mid = rest.astype(BF16)
    low = (rest - mid.astype(F32)).astype(BF16)
    parts = jnp.concatenate([hi, mid, low], axis=0)
    column = lax.broadcasted_iota(jnp.int32, (1024, 1024), 0)
    target = lax.broadcasted_iota(jnp.int32, (1024, 1024), 1)
    permute = jnp.where(column == 8 * (target % 128) + target // 128, 1.0, 0.0).astype(BF16)
    moved = jnp.dot(parts, permute, preferred_element_type=F32)
    moved = (moved[0:16] + moved[16:32]) + moved[32:48]
    for h in range(8):
        weights[16 * h : 16 * h + 16, :] = moved[:, 128 * h : 128 * h + 128]

    lane = lax.broadcasted_iota(jnp.int32, (1024, 128), 1)
    depth = lax.broadcasted_iota(jnp.int32, (1024, 128), 0)
    pick0 = jnp.where(depth == 64 * lane, 1.0, 0.0).astype(BF16)
    pick1 = jnp.where(depth == 64 * (lane - 16), 1.0, 0.0).astype(BF16)
    pieces = []
    for q in range(4):
        loads[q].wait()
        for i in range(4 * q, 4 * q + 4):
            rows = [rec[p, 64 * i : 64 * i + 8, :].astype(F32)[0:1] for p in range(2)]
            send1[i] = jnp.concatenate(rows, axis=0).astype(BF16)
    for q in range(4):
        span = slice(q * chunk, q * chunk + chunk)
        columns = jnp.dot(rec[0, span, :], pick0, preferred_element_type=F32)
        columns += jnp.dot(rec[1, span, :], pick1, preferred_element_type=F32)
        turned = columns.T
        pieces.append(turned[0:32])
    local = jnp.concatenate(pieces, axis=1).astype(BF16)
    lbuf[r, 0] = local[0:16]
    lbuf[r, 1] = local[16:32]

    pl.semaphore_wait(barrier, len(peers))

    def remote(src, dst, send_sem, recv_sem, device):
        copy = pltpu.make_async_remote_copy(
            src_ref=src, dst_ref=dst, send_sem=send_sem, recv_sem=recv_sem, device_id=device, device_id_type=MESH
        )
        copy.start()
        return copy

    sent = []
    order = [8, 9, 7, 6, 10, 11, 5, 4, 12, 13, 3, 2, 14, 15, 1]
    for n, d in enumerate(order):
        other = lax.rem(r + d, NR)
        sent.append(remote(send1.at[other], recv1.at[r], s1_sem.at[n], r1_sem.at[r], to_rcv(other)))
    recv1[r] = send1[r]

    lcount = [0]

    def left_send(owner, h, target):
        n = lcount[0]
        lcount[0] += 1
        sent.append(remote(lbuf.at[owner, h], lbuf.at[owner, h], ls_sem.at[n], lr_sem.at[owner, h], to_rcv(target)))

    def left_wait(owner, h):
        pltpu.make_async_copy(lbuf.at[owner, h], lbuf.at[owner, h], lr_sem.at[owner, h]).wait()

    z_up, z_down = rcv_of(z + 1, xh), rcv_of(z - 1, xh)
    far = rcv_of(z, 1 - xh)
    for h in range(2):
        left_send(r, h, far)
    for h in range(2):
        left_send(r, h, z_up)
        left_send(r, h, z_down)

    def left_round(dist, x):
        for h in range(2):
            if dist < 4 or h == 0:
                left_wait(rcv_of(z - dist, x), h)
                if dist + 1 < 4 or (dist + 1 == 4 and h == 0):
                    left_send(rcv_of(z - dist, x), h, z_up)
            if dist < 4 or h == 1:
                left_wait(rcv_of(z + dist, x), h)
                if dist + 1 < 4 or (dist + 1 == 4 and h == 1):
                    left_send(rcv_of(z + dist, x), h, z_down)

    for h in range(2):
        left_wait(far, h)
        left_send(far, h, z_up)
        left_send(far, h, z_down)
    left_round(1, xh)

    for d in range(1, NR):
        other = lax.rem(r + d, NR)
        pltpu.make_async_copy(recv1.at[other], recv1.at[other], r1_sem.at[other]).wait()
    rows = recv1[...].astype(F32).reshape(32, 1024)
    x = jnp.concatenate([rows[:, 128 * j : 128 * j + 128] for j in range(8)], axis=0)
    cos, sin = twi_ref[0], twi_ref[1]
    a = jnp.dot(dft_ref[0], x, precision=HIGHEST, preferred_element_type=F32)
    ar, ai = a[0:128], a[128:256]
    b = jnp.concatenate([ar * cos + ai * sin, ai * cos - ar * sin], axis=1)
    b = jnp.dot(b, dft_ref[1], precision=HIGHEST, preferred_element_type=F32)
    w = weights[...]
    b = b * jnp.concatenate([w, w], axis=1)
    b = jnp.dot(b, dft_ref[2], precision=HIGHEST, preferred_element_type=F32)
    ur, ui = b[:, 0:128], b[:, 128:256]
    u = jnp.concatenate([ur * cos - ui * sin, ui * cos + ur * sin], axis=0)
    out = jnp.dot(dft_ref[3], u, precision=HIGHEST, preferred_element_type=F32)

    rounded = out.astype(BF16)
    rho = lax.broadcasted_iota(jnp.int32, (256, 512), 0)
    goal = lax.broadcasted_iota(jnp.int32, (256, 512), 1)
    place = (rho & 1) * 256 + 2 * (8 * ((rho >> 1) & 15) + (rho >> 5))
    sampled = None
    for e in range(2):
        choose = jnp.where(goal == place + e, 1.0, 0.0).astype(BF16)
        got = lax.dot_general(rounded, choose, (((0,), (0,)), ((), ())), preferred_element_type=F32)
        got = got[64 * e : 64 * e + 1]
        sampled = got if sampled is None else sampled + got
    sampled = jnp.concatenate([sampled[:, 0:256], sampled[:, 256:512]], axis=0)
    spread = jnp.concatenate([out[32 * j : 32 * j + 32] for j in range(8)], axis=1)
    for i in range(NR):
        send2[i] = jnp.concatenate([spread[2 * i : 2 * i + 2], sampled], axis=1).astype(BF16)

    for n, d in enumerate(order):
        other = lax.rem(r + d, NR)
        sent.append(remote(send2.at[other], recv2.at[r], s2_sem.at[n], r2_sem.at[r], to_rcv(other)))
    recv2[r] = send2[r]

    left_round(1, 1 - xh)
    left_round(2, xh)
    left_round(2, 1 - xh)

    for d in range(1, NR):
        other = lax.rem(r + d, NR)
        pltpu.make_async_copy(recv2.at[other], recv2.at[other], r2_sem.at[other]).wait()
    got = recv2[...].astype(F32)
    fbuf[s, 0] = got[:, 0, :].astype(BF16)
    fbuf[s, 1] = got[:, 1, :].astype(BF16)

    fcount = [0]

    def filt_send(owner, h, target):
        n = fcount[0]
        fcount[0] += 1
        sent.append(remote(fbuf.at[owner, h], fbuf.at[owner, h], fs_sem.at[n], fr_sem.at[owner, h], to_src(target)))

    def filt_wait(owner, h):
        pltpu.make_async_copy(fbuf.at[owner, h], fbuf.at[owner, h], fr_sem.at[owner, h]).wait()

    for h in range(2):
        filt_send(s, h, x_peer)
    for h in range(2):
        filt_send(s, h, up)
        filt_send(s, h, down)
        filt_send(s, h, mate)
    left_round(3, xh)
    left_round(3, 1 - xh)
    for h in range(2):
        filt_wait(x_peer, h)
        for target in (up, down, mate):
            filt_send(x_peer, h, target)
    left_round(4, xh)
    left_round(4, 1 - xh)
    for x in (xl, 1 - xl):
        for h in range(2):
            below, above = src_of(x, y - 1, c), src_of(x, y + 1, c)
            filt_wait(below, h)
            if h == 0:
                filt_send(below, h, up)
            filt_send(below, h, mate)
            filt_wait(above, h)
            if h == 1:
                filt_send(above, h, down)
            filt_send(above, h, mate)

    for p in range(2):
        for g in range(2):
            part = lbuf[8 * g : 8 * g + 8, p].reshape(128, ROWS)
            lnat[:, 256 * p + 128 * g : 256 * p + 128 * g + 128] = part.astype(F32).T.astype(BF16)
    left_out = pltpu.make_async_copy(lnat, left_hbm, out_sem.at[0])
    left_out.start()

    for x in (xl, 1 - xl):
        for h in range(2):
            opposite = src_of(x, y + 2, c)
            filt_wait(opposite, h)
            filt_send(opposite, h, mate)
    for x in range(2):
        for yy in range(4):
            for h in range(2):
                filt_wait(src_of(x, yy, 1 - c), h)
    filt_out = pltpu.make_async_copy(fbuf, filt_hbm, out_sem.at[1])
    filt_out.start()
    for copy in sent:
        copy.wait_send()
    left_out.wait()
    filt_out.wait()


def gather(recorded, obliquity):
    dft, twiddle = tables()
    vmem = pl.BlockSpec(memory_space=pltpu.VMEM)
    anywhere = pl.BlockSpec(memory_space=pl.ANY)
    dma = pltpu.SemaphoreType.DMA
    return pl.pallas_call(
        gather_kernel,
        out_shape=(
            jax.ShapeDtypeStruct((ROWS, 2 * K), BF16),
            jax.ShapeDtypeStruct((NS, 2, 16, WIDE), BF16),
        ),
        in_specs=[anywhere, vmem, vmem, vmem],
        out_specs=(anywhere, anywhere),
        scratch_shapes=[
            pltpu.VMEM((2, ROWS, COLS), BF16),
            pltpu.VMEM((NR, 2, COLS), BF16),
            pltpu.VMEM((NR, 2, COLS), BF16),
            pltpu.VMEM((NR, 2, WIDE), BF16),
            pltpu.VMEM((NR, 2, WIDE), BF16),
            pltpu.VMEM((NR, 2, 16, ROWS), BF16),
            pltpu.VMEM((NS, 2, 16, WIDE), BF16),
            pltpu.VMEM((ROWS, 2 * K), BF16),
            pltpu.VMEM((128, 128), F32),
            dma((4,)),
            dma((2,)),
            dma((NR,)),
            dma((NR,)),
            dma((NR,)),
            dma((NR,)),
            dma((32,)),
            dma((NR, 2)),
            dma((32,)),
            dma((NS, 2)),
        ],
        compiler_params=pltpu.CompilerParams(
            collective_id=0, has_side_effects=True, vmem_limit_bytes=40 * 2**20
        ),
        name="gather",
    )(recorded, obliquity, jnp.asarray(dft), jnp.asarray(twiddle))


TM = 128


def update_kernel(rec_ref, left_ref, filt_ref, clip_ref, first_ref, second_ref, right, sampled):
    step = pl.program_id(0)

    @pl.when(step == 0)
    def _():
        for p, places in ((0, (256,)), (1, (0,))):
            value = filt_ref[:, p].reshape(K, WIDE)
            for place in places:
                right[place : place + K, :] = value[:, :COLS]
                sampled[place : place + K, :] = value[:, COLS:]
            if p == 1:
                right[512:768, :] = -value[:, :COLS]
                sampled[512:768, :] = -value[:, COLS:]

    clip = jnp.broadcast_to(clip_ref[pl.ds(step, 1), :], (128, 128)).T
    scale = 1.0 / (clip * clip)
    scale = jnp.concatenate([scale, scale], axis=1)

    def limited(left, table, span):
        real = jnp.dot(left, table[256:768, span], preferred_element_type=F32)
        imag = jnp.dot(left, table[0:512, span], preferred_element_type=F32)
        limiter = lax.rsqrt(1.0 + (real * real + imag * imag) * scale)
        return real * limiter, imag * limiter

    left = left_ref[...]
    real, imag = limited(left, sampled, slice(0, 256))
    left2 = jnp.concatenate(
        [
            (left[:, 0:256].astype(F32) - real).astype(BF16),
            (left[:, 256:512].astype(F32) - imag).astype(BF16),
        ],
        axis=1,
    )
    for q in range(COLS // 256):
        span = slice(256 * q, 256 * q + 256)
        base = [rec_ref[p, :, span].astype(F32) for p in range(2)]
        for rows, out in ((left, first_ref), (left2, second_ref)):
            real, imag = limited(rows, right, span)
            out[0, :, span] = (base[0] - real).astype(BF16)
            out[1, :, span] = (base[1] - imag).astype(BF16)


def update(recorded, left, filtered, clip_level):
    block = pl.BlockSpec((2, TM, COLS), lambda i: (0, i, 0))
    once = dict(pipeline_mode=pl.Buffered(1))
    out = jax.ShapeDtypeStruct((2, ROWS, COLS), BF16)
    return pl.pallas_call(
        update_kernel,
        out_shape=(out, out),
        grid=(ROWS // TM,),
        in_specs=[
            block,
            pl.BlockSpec((TM, 2 * K), lambda i: (i, 0)),
            pl.BlockSpec((NS, 2, 16, WIDE), lambda i: (0, 0, 0, 0), **once),
            pl.BlockSpec((ROWS // 128, 128), lambda i: (0, 0), **once),
        ],
        out_specs=(block, block),
        scratch_shapes=[pltpu.VMEM((3 * K, COLS), BF16), pltpu.VMEM((3 * K, K), BF16)],
        compiler_params=pltpu.CompilerParams(vmem_limit_bytes=40 * 2**20),
        name="update",
    )(recorded, left, filtered, clip_level)


def per_device(recorded, obliquity, clip_level):
    left, filtered = gather(recorded, obliquity)
    return update(recorded, left, filtered, clip_level.reshape(ROWS // 128, 128))


def solution(mesh):
    return jax.shard_map(
        per_device,
        mesh=mesh,
        in_specs=(P(None, "src", "rcv"), P(), P("src")),
        out_specs=(P(None, "src", "rcv"), P(None, "src", "rcv")),
        check_vma=False,
    )
```

time: 452 us -> 54.8 us (0.12); the launches traced: 444 us -> 54.6 us
  other arithmetic: 179 us -> 0 us
  waiting for transfers between devices: 104 us -> 0 us
  local copies, waits for them, and re-layouts: 80.5 us -> 5.15 us
  Pallas kernels: 0 us -> 48.8 us
  matrix products: 36.3 us -> 0 us
  blocking collectives: 18.3 us -> 0 us
  between operations: 14.2 us -> 0.66 us
  starting transfers between devices: 11.9 us -> 0 us
    unnamed x2 -> x0, other arithmetic: 116 us -> none
    all_gather x3 -> x0, waiting for transfers between devices: 104 us -> none  [the longest x2 74.2 us: per_device(): left_panel = lax.all_gather(left_local, 'rcv', axis=1, tiled=True)]
    pallas_call x0 -> x2, Pallas kernels: none -> 48.8 us  [the longest x1 38.6 us: gather(): pl.pallas_call(gather_kernel, out_shape=(jax.ShapeDtypeStruct((ROWS, 2 *...]
    dot_general x12 -> x0, matrix products: 36.3 us -> none  [the longest x2 28.2 us: long_transform(): jnp.dot(joined.reshape(-1, 2 * length), long_table(length, orient), preci...]
    another operation x2 -> x0, local copies, waits for them, and re-layouts: 23.2 us -> none  [filter_rows(): returned = jnp.stack([real_part * inverse_scale, imag_part * inverse_scale])]
    unnamed x15 -> x10, local copies, waits for them, and re-layouts: 27.8 us -> 5.15 us
    all_to_all x1 -> x0, blocking collectives: 18.3 us -> none  [through_rows(): lax.all_to_all(returned, 'rcv', split_axis=2, concat_axis=1, tiled=True)]
    mul x3 -> x0, other arithmetic: 17.7 us -> none  [the longest x1 17.6 us: long_table(): sine_part = orient * jnp.sin(angles)]
  transfers between devices with their start and end apart: 4 -> 0, of which waited for: 2 -> 0; matrix products, arithmetic and copies ran while one was open for 60% -> 0% of each run, Pallas kernels for 0% -> 0%
where the time goes in v1:
time: 54.8 us; the launch traced here: 54.6 us
  Pallas kernels  48.8 us (89%)
  local copies, waits for them, and re-layouts  5.15 us (9%)
  between operations  0.66 us (1%)
    pallas_call x1, Pallas kernels, gather(): pl.pallas_call(gather_kernel, out_shape=(jax.ShapeDtypeStruct((ROWS, 2 *...  38.6 us
    pallas_call x1, Pallas kernels, update(): pl.pallas_call(update_kernel, out_shape=(out, out), grid=(ROWS // TM,), i...  10.2 us
    unnamed x10, local copies, waits for them, and re-layouts  5.15 us

profile of v1, /device:TPU:1, one launch (start us, length us, event | category | flops | bytes accessed | tf_op | source)
XLA Modules:
  0.0 54.6 jit_solution(485861176546539923)
XLA Ops:
  0.6 0.0 copy-start
  0.6 2.2 %copy-done = bf16[2,1024,1024]{2,1,0:T(8,128)(2,1)S(1)} copy-done((bf16[2,1024,1024]{2,1,0:T(8,128)(2,1)S(1)}, bf16[2,1024,1024]{2,1,0:T(8,128)(2,1)}, u32[]{:S(2)}) %copy-start) | copy-done | bytes 4194328
  2.8 0.0 copy-start.1
  2.8 1.2 %copy-done.1 = f32[4,256,256]{2,1,0:T(8,128)S(1)} copy-done((f32[4,256,256]{2,1,0:T(8,128)S(1)}, f32[4,256,256]{2,1,0:T(8,128)}, u32[]{:S(2)}) %copy-start.1) | copy-done | bytes 1048600
  4.0 0.0 copy-start.2
  4.0 0.9 %copy-done.2 = f32[2,128,128]{2,1,0:T(8,128)S(1)} copy-done((f32[2,128,128]{2,1,0:T(8,128)S(1)}, f32[2,128,128]{2,1,0:T(8,128)}, u32[]{:S(2)}) %copy-start.2) | copy-done | bytes 131096
  4.9 0.0 copy-start.3
  5.0 0.8 %copy-done.3 = f32[16,1024]{1,0:T(8,128)S(1)} copy-done((f32[16,1024]{1,0:T(8,128)S(1)}, f32[16,1024]{1,0:T(8,128)}, u32[]{:S(2)}) %copy-start.3) | copy-done | bytes 65560
  5.8 0.0 copy-start.4
  5.8 38.6 %gather.1 = (bf16[1024,512]{1,0:T(8,128)(2,1)S(1)}, bf16[16,2,16,1280]{3,2,1,0:T(8,128)(2,1)S(1)}) custom-call(bf16[2,1024,1024]{2,1,0:T(8,128)(2,1)S(1)} %copy-done, f32[16,1024]{1,0:T(8,128)S(1)} %copy-done.3, f32[4,256,256]{2,1,0:T(8,128)S(1)} %copy-done.1, f32[2,128,128]{2,1,0:T(8,128)S(1)} %copy-done.2), custom_call_target="tpu_custom_call" | custom-call | tf_op jit(solution)/shard_map/gather/pallas_call | solution.py:282
  44.4 0.0 copy-done.4
  44.4 10.2 %update.1 = (bf16[2,1024,1024]{2,1,0:T(8,128)(2,1)}, bf16[2,1024,1024]{2,1,0:T(8,128)(2,1)}) custom-call(bf16[2,1024,1024]{2,1,0:T(8,128)(2,1)S(1)} %copy-done, bf16[1024,512]{1,0:T(8,128)(2,1)S(1)} %get-tuple-element.4.left_ref, bf16[16,2,16,1280]{3,2,1,0:T(8,128)(2,1)S(1)} %get-tuple-element.5.filt_ref, f32[8,128]{1,0:T(8,128)S(1)} %bitcast.1), custom_call_target="tpu_custom_call" | custom-call | tf_op jit(solution)/shard_map/update/pallas_call | solution.py:367
Async XLA Ops:
  0.6 2.2 %copy-start = (bf16[2,1024,1024]{2,1,0:T(8,128)(2,1)S(1)}, bf16[2,1024,1024]{2,1,0:T(8,128)(2,1)}, u32[]{:S(2)}) copy-start(bf16[2,1024,1024]{2,1,0:T(8,128)(2,1)} %rec_ref.1) | copy-start | bytes 12582916
  2.8 1.2 %copy-start.1 = (f32[4,256,256]{2,1,0:T(8,128)S(1)}, f32[4,256,256]{2,1,0:T(8,128)}, u32[]{:S(2)}) copy-start(f32[4,256,256]{2,1,0:T(8,128)} %constant.4.clone.dft_ref) | copy-start | bytes 3145732
  4.0 0.9 %copy-start.2 = (f32[2,128,128]{2,1,0:T(8,128)S(1)}, f32[2,128,128]{2,1,0:T(8,128)}, u32[]{:S(2)}) copy-start(f32[2,128,128]{2,1,0:T(8,128)} %constant.5.clone.twi_ref) | copy-start | bytes 393220
  4.9 0.8 %copy-start.3 = (f32[16,1024]{1,0:T(8,128)S(1)}, f32[16,1024]{1,0:T(8,128)}, u32[]{:S(2)}) copy-start(f32[16,1024]{1,0:T(8,128)} %obl_ref.1) | copy-start | bytes 196612
  5.8 38.6 %copy-start.4 = (f32[1024]{0:T(1024)S(1)}, f32[1024]{0:T(1024)}, u32[]{:S(2)}) copy-start(f32[1024]{0:T(1024)} %param.7) | copy-start | bytes 12292

commit v2 on v1

v2 whole, which is shorter than its diff:
```python
import functools

import jax
import jax.numpy as jnp
import numpy as np
from jax import lax
from jax.experimental import pallas as pl
from jax.experimental.pallas import tpu as pltpu
from jax.sharding import PartitionSpec as P

N = 16384
K = 256
MESH = pl.DeviceIdType.MESH
F32 = jnp.float32
BF16 = jnp.bfloat16
HIGHEST = lax.Precision.HIGHEST
NR = 16
NS = 16
ROWS = 1024
COLS = 1024
WIDE = COLS + K


def tables():
    k1 = np.arange(128)
    rho = np.arange(256)
    n1 = 8 * ((rho >> 1) & 15) + (rho >> 5)
    part = rho & 1
    theta = 2 * np.pi * ((k1[:, None] * n1[None, :]) % 128) / 128
    cos, sin = np.cos(theta), np.sin(theta)
    even = part[None, :] == 0
    m1 = np.concatenate([np.where(even, cos, sin), np.where(even, -sin, cos)], axis=0)
    m4 = np.concatenate([np.where(even, cos, sin).T, np.where(even, -sin, cos).T], axis=1)
    angle = 2 * np.pi * ((k1[:, None] * k1[None, :]) % 128) / 128
    cos, sin = np.cos(angle), np.sin(angle)
    m2 = np.block([[cos, -sin], [sin, cos]])
    m3 = np.block([[cos, sin], [-sin, cos]])
    phi = 2 * np.pi * (k1[:, None] * k1[None, :]) / N
    twiddle = np.stack([np.cos(phi), np.sin(phi)])
    return np.stack([m1, m2, m3, m4]).astype(np.float32), twiddle.astype(np.float32)


def gather_kernel(
    rec_hbm, obl_hbm, dft_hbm, twi_hbm, left_hbm, filt_hbm,
    rec, rows_buf, obl_ref, dft_ref, twi_ref, send1, recv1, send2, recv2, lbuf, fbuf, lnat, weights,
    rec_sem, out_sem, s1_sem, r1_sem, s2_sem, r2_sem, ls_sem, lr_sem, fs_sem, fr_sem, fm_sem,
):
    s = lax.axis_index("src")
    r = lax.axis_index("rcv")
    z, xh = r // 2, lax.rem(r, 2)
    xl, y, c = s // 8, lax.rem(s // 2, 4), lax.rem(s, 2)

    def src_of(x, yy, core):
        return x * 8 + lax.rem(yy + 8, 4) * 2 + core

    def rcv_of(zz, x):
        return lax.rem(zz + 16, 8) * 2 + x

    def to_rcv(index):
        return (s, index)

    def to_src(index):
        return (index, r)

    peers = [to_rcv(lax.rem(r + d, NR)) for d in range(1, NR)]
    x_peer = src_of(1 - xl, y, c)
    up, down = src_of(xl, y + 1, c), src_of(xl, y - 1, c)
    mate = src_of(xl, y, 1 - c)
    diag_up, diag_down = src_of(1 - xl, y + 1, c), src_of(1 - xl, y - 1, c)
    peers += [to_src(i) for i in (x_peer, up, down, mate, diag_up, diag_down)]

    barrier = pltpu.get_barrier_semaphore()
    for peer in peers:
        pl.semaphore_signal(barrier, inc=1, device_id=peer, device_id_type=MESH)

    constants = [
        pltpu.make_async_copy(obl_hbm, obl_ref, rec_sem.at[5]),
        pltpu.make_async_copy(dft_hbm, dft_ref, rec_sem.at[6]),
        pltpu.make_async_copy(twi_hbm, twi_ref, rec_sem.at[7]),
    ]
    constants[0].start()
    heads = pltpu.make_async_copy(rec_hbm.at[:, :, pl.ds(0, 8), :], rows_buf, rec_sem.at[4])
    heads.start()
    chunk = ROWS // 4
    loads = []
    for q in range(4):
        load = pltpu.make_async_copy(
            rec_hbm.at[:, pl.ds(4 * q, 4), :, :], rec.at[:, pl.ds(4 * q, 4), :, :], rec_sem.at[q]
        )
        load.start()
        loads.append(load)
    for load in constants[1:]:
        load.start()

    with jax.named_scope("rows"):
        heads.wait()
        for i in range(NR):
            rows = [rows_buf[p, i].astype(F32)[0:1] for p in range(2)]
            send1[i] = jnp.concatenate(rows, axis=0).astype(BF16)

    with jax.named_scope("barrier"):
        pl.semaphore_wait(barrier, len(peers))

    def remote(src, dst, send_sem, recv_sem, device):
        copy = pltpu.make_async_remote_copy(
            src_ref=src, dst_ref=dst, send_sem=send_sem, recv_sem=recv_sem, device_id=device, device_id_type=MESH
        )
        copy.start()

    def drain(buffer, sem, blocks=15):
        pltpu.make_async_copy(buffer.at[pl.ds(0, blocks)], buffer.at[pl.ds(0, blocks)], sem).wait()

    order = [8, 9, 7, 6, 10, 11, 5, 4, 12, 13, 3, 2, 14, 15, 1]
    for d in order:
        other = lax.rem(r + d, NR)
        remote(send1.at[other], recv1.at[r], s1_sem, r1_sem, to_rcv(other))
    recv1[r] = send1[r]

    with jax.named_scope("select"):
        lane = lax.broadcasted_iota(jnp.int32, (1024, 128), 1)
        depth = lax.broadcasted_iota(jnp.int32, (1024, 128), 0)
        pick0 = jnp.where(depth == 64 * lane, 1.0, 0.0).astype(BF16)
        pick1 = jnp.where(depth == 64 * (lane - 16), 1.0, 0.0).astype(BF16)
        pieces = []
        for q in range(4):
            loads[q].wait()
            columns = jnp.dot(rec[0, 4 * q : 4 * q + 4].reshape(chunk, COLS), pick0, preferred_element_type=F32)
            columns += jnp.dot(rec[1, 4 * q : 4 * q + 4].reshape(chunk, COLS), pick1, preferred_element_type=F32)
            turned = columns.T
            pieces.append(turned[0:32])
        local = jnp.concatenate(pieces, axis=1).astype(BF16)
        lbuf[r, 0] = local[0:16]
        lbuf[r, 1] = local[16:32]

    def left_send(owner, h, target):
        remote(lbuf.at[owner, h], lbuf.at[owner, h], ls_sem, lr_sem.at[owner, h], to_rcv(target))

    def left_wait(owner, h):
        pltpu.make_async_copy(lbuf.at[owner, h], lbuf.at[owner, h], lr_sem.at[owner, h]).wait()

    z_up, z_down = rcv_of(z + 1, xh), rcv_of(z - 1, xh)
    far = rcv_of(z, 1 - xh)
    for h in range(2):
        left_send(r, h, far)
    for h in range(2):
        left_send(r, h, z_up)
        left_send(r, h, z_down)

    def left_round(dist, x):
        for h in range(2):
            if dist < 4 or h == 0:
                left_wait(rcv_of(z - dist, x), h)
                if dist + 1 < 4 or (dist + 1 == 4 and h == 0):
                    left_send(rcv_of(z - dist, x), h, z_up)
            if dist < 4 or h == 1:
                left_wait(rcv_of(z + dist, x), h)
                if dist + 1 < 4 or (dist + 1 == 4 and h == 1):
                    left_send(rcv_of(z + dist, x), h, z_down)

    with jax.named_scope("weights"):
        constants[0].wait()
        obl = obl_ref[...] * (1.0 / N)
        hi = obl.astype(BF16)
        rest = obl - hi.astype(F32)
        mid = rest.astype(BF16)
        low = (rest - mid.astype(F32)).astype(BF16)
        parts = jnp.concatenate([hi, mid, low], axis=0)
        column = lax.broadcasted_iota(jnp.int32, (1024, 1024), 0)
        target = lax.broadcasted_iota(jnp.int32, (1024, 1024), 1)
        permute = jnp.where(column == 8 * (target % 128) + target // 128, 1.0, 0.0).astype(BF16)
        moved = jnp.dot(parts, permute, preferred_element_type=F32)
        moved = (moved[0:16] + moved[16:32]) + moved[32:48]
        for h in range(8):
            weights[16 * h : 16 * h + 16, :] = moved[:, 128 * h : 128 * h + 128]

    with jax.named_scope("wait1"):
        drain(recv1, r1_sem)

    with jax.named_scope("left1"):
        left_round(1, xh)

    with jax.named_scope("dft"):
        for load in constants[1:]:
            load.wait()
        rows = recv1[...].astype(F32).reshape(32, 1024)
        x = jnp.concatenate([rows[:, 128 * j : 128 * j + 128] for j in range(8)], axis=0)
        cos, sin = twi_ref[0], twi_ref[1]
        a = jnp.dot(dft_ref[0], x, precision=HIGHEST, preferred_element_type=F32)
        ar, ai = a[0:128], a[128:256]
        b = jnp.concatenate([ar * cos + ai * sin, ai * cos - ar * sin], axis=1)
        b = jnp.dot(b, dft_ref[1], precision=HIGHEST, preferred_element_type=F32)

    with jax.named_scope("far"):
        for h in range(2):
            left_wait(far, h)
            left_send(far, h, z_up)
            left_send(far, h, z_down)

    with jax.named_scope("dft2"):
        w = weights[...]
        b = b * jnp.concatenate([w, w], axis=1)
        b = jnp.dot(b, dft_ref[2], precision=HIGHEST, preferred_element_type=F32)
        ur, ui = b[:, 0:128], b[:, 128:256]
        u = jnp.concatenate([ur * cos - ui * sin, ui * cos + ur * sin], axis=0)
        out = jnp.dot(dft_ref[3], u, precision=HIGHEST, preferred_element_type=F32)

    with jax.named_scope("pack"):
        rounded = out.astype(BF16)
        rho = lax.broadcasted_iota(jnp.int32, (256, 512), 0)
        goal = lax.broadcasted_iota(jnp.int32, (256, 512), 1)
        place = (rho & 1) * 256 + 2 * (8 * ((rho >> 1) & 15) + (rho >> 5))
        sampled = None
        for e in range(2):
            choose = jnp.where(goal == place + e, 1.0, 0.0).astype(BF16)
            got = lax.dot_general(rounded, choose, (((0,), (0,)), ((), ())), preferred_element_type=F32)
            got = got[64 * e : 64 * e + 1]
            sampled = got if sampled is None else sampled + got
        sampled = jnp.concatenate([sampled[:, 0:256], sampled[:, 256:512]], axis=0)
        spread = jnp.concatenate([out[32 * j : 32 * j + 32] for j in range(8)], axis=1)
        for i in range(NR):
            send2[i] = jnp.concatenate([spread[2 * i : 2 * i + 2], sampled], axis=1).astype(BF16)

    for d in order:
        other = lax.rem(r + d, NR)
        remote(send2.at[other], recv2.at[r], s2_sem, r2_sem, to_rcv(other))
    recv2[r] = send2[r]

    with jax.named_scope("left2"):
        left_round(2, xh)
        left_round(1, 1 - xh)

    with jax.named_scope("wait2"):
        drain(recv2, r2_sem)

    with jax.named_scope("unpack"):
        got = recv2[...].astype(F32)
        fbuf[s, 0] = got[:, 0, :].astype(BF16)
        fbuf[s, 1] = got[:, 1, :].astype(BF16)

    def filt_send(owner, h, target):
        remote(fbuf.at[owner, h], fbuf.at[owner, h], fs_sem, fr_sem.at[owner // 2, h], to_src(target))

    def filt_mate(owner, h):
        remote(fbuf.at[owner, h], fbuf.at[owner, h], fs_sem, fm_sem, to_src(mate))

    def filt_wait(owner, h):
        pltpu.make_async_copy(fbuf.at[owner, h], fbuf.at[owner, h], fr_sem.at[owner // 2, h]).wait()

    for h in range(2):
        filt_send(s, h, diag_up if h == 0 else diag_down)
        filt_send(s, h, up if h == 0 else down)
        filt_mate(s, h)
    for h in range(2):
        filt_send(s, h, diag_down if h == 0 else diag_up)
        filt_send(s, h, down if h == 0 else up)
    for h in range(2):
        filt_send(s, h, x_peer)

    def filt_near(x):
        below, above = src_of(x, y - 1, c), src_of(x, y + 1, c)
        filt_wait(below, 0)
        filt_send(below, 0, up)
        filt_mate(below, 0)
        filt_wait(above, 1)
        filt_send(above, 1, down)
        filt_mate(above, 1)
        for owner, h in ((below, 1), (above, 0)):
            filt_wait(owner, h)
            filt_mate(owner, h)

    def filt_last(owner):
        for h in range(2):
            filt_wait(owner, h)
            filt_mate(owner, h)

    with jax.named_scope("left3"):
        left_round(3, xh)
        left_round(2, 1 - xh)

    with jax.named_scope("filt1"):
        filt_near(xl)

    with jax.named_scope("left4"):
        left_round(4, xh)
        left_round(3, 1 - xh)

    with jax.named_scope("filt2"):
        filt_near(1 - xl)

    with jax.named_scope("filt3"):
        filt_last(src_of(xl, y + 2, c))
        filt_last(x_peer)

    with jax.named_scope("filt4"):
        filt_last(src_of(1 - xl, y + 2, c))

    with jax.named_scope("left5"):
        left_round(4, 1 - xh)

    with jax.named_scope("turn"):
        for p in range(2):
            for g in range(2):
                part = lbuf[8 * g : 8 * g + 8, p].reshape(128, ROWS)
                lnat[:, 256 * p + 128 * g : 256 * p + 128 * g + 128] = part.astype(F32).T.astype(BF16)

    left_out = pltpu.make_async_copy(lnat, left_hbm, out_sem.at[0])
    left_out.start()

    with jax.named_scope("store"):
        def filt_store(owner):
            pltpu.make_async_copy(fbuf.at[owner], filt_hbm.at[owner], out_sem.at[1]).start()

        for x in range(2):
            for yy in range(4):
                filt_store(src_of(x, yy, c))
        drain(fbuf, fm_sem, 8)
        for x in range(2):
            for yy in range(4):
                filt_store(src_of(x, yy, 1 - c))

    with jax.named_scope("drain"):
        drain(send1, s1_sem)
        drain(send2, s2_sem)
        drain(lbuf, ls_sem)
        drain(fbuf, fs_sem)
        left_out.wait()
        drain(fbuf, out_sem.at[1], 16)


def gather(recorded, obliquity):
    dft, twiddle = tables()
    hbm = pl.BlockSpec(memory_space=pltpu.HBM)
    anywhere = pl.BlockSpec(memory_space=pl.ANY)
    dma = pltpu.SemaphoreType.DMA
    return pl.pallas_call(
        gather_kernel,
        out_shape=(
            jax.ShapeDtypeStruct((ROWS, 2 * K), BF16),
            jax.ShapeDtypeStruct((NS, 2, 16, WIDE), BF16),
        ),
        in_specs=[hbm] * 4,
        out_specs=(anywhere, anywhere),
        scratch_shapes=[
            pltpu.VMEM((2, 16, 64, COLS), BF16),
            pltpu.VMEM((2, 16, 8, COLS), BF16),
            pltpu.VMEM((16, 1024), F32),
            pltpu.VMEM((4, 256, 256), F32),
            pltpu.VMEM((2, 128, 128), F32),
            pltpu.VMEM((NR, 2, COLS), BF16),
            pltpu.VMEM((NR, 2, COLS), BF16),
            pltpu.VMEM((NR, 2, WIDE), BF16),
            pltpu.VMEM((NR, 2, WIDE), BF16),
            pltpu.VMEM((NR, 2, 16, ROWS), BF16),
            pltpu.VMEM((NS, 2, 16, WIDE), BF16),
            pltpu.VMEM((ROWS, 2 * K), BF16),
            pltpu.VMEM((128, 128), F32),
            dma((8,)),
            dma((2,)),
            dma,
            dma,
            dma,
            dma,
            dma,
            dma((NR, 2)),
            dma,
            dma((NS // 2, 2)),
            dma,
        ],
        compiler_params=pltpu.CompilerParams(
            collective_id=0, has_side_effects=True, vmem_limit_bytes=60 * 2**20
        ),
        name="gather",
    )(recorded.reshape(2, 16, 64, COLS), obliquity, jnp.asarray(dft), jnp.asarray(twiddle))


TC = 256
CHUNK = 256


def update_kernel(rec_ref, left_ref, filt_ref, clip_ref, first_ref, second_ref, left2, scale, minus):
    step = pl.program_id(0)

    @pl.when(step == 0)
    def _():
        for g in range(ROWS // 128):
            clip = jnp.broadcast_to(clip_ref[g : g + 1, :], (128, 128)).T
            scale[128 * g : 128 * g + 128, :] = 1.0 / (clip * clip)

    real_rows = filt_ref[:, 0].reshape(K, TC)
    imag_rows = filt_ref[:, 1].reshape(K, TC)
    minus[...] = -imag_rows
    to_real = jnp.concatenate([real_rows, minus[...]], axis=0)
    to_imag = jnp.concatenate([imag_rows, real_rows], axis=0)

    def limited(left, rows):
        real = jnp.dot(left, to_real, preferred_element_type=F32)
        imag = jnp.dot(left, to_imag, preferred_element_type=F32)
        part = scale[rows, :]
        part = jnp.concatenate([part] * (TC // 128), axis=1)
        limiter = lax.rsqrt(1.0 + (real * real + imag * imag) * part)
        return real * limiter, imag * limiter

    @pl.when(step == 0)
    def _():
        for g in range(ROWS // CHUNK):
            rows = slice(CHUNK * g, CHUNK * g + CHUNK)
            real, imag = limited(left_ref[rows, :], rows)
            left2[rows, 0:K] = (left_ref[rows, 0:K].astype(F32) - real).astype(BF16)
            left2[rows, K : 2 * K] = (left_ref[rows, K : 2 * K].astype(F32) - imag).astype(BF16)

    @pl.when(step > 0)
    def _():
        for g in range(ROWS // CHUNK):
            rows = slice(CHUNK * g, CHUNK * g + CHUNK)
            for left, out in ((left_ref, first_ref), (left2, second_ref)):
                real, imag = limited(left[rows, :], rows)
                out[0, rows, :] = (rec_ref[0, rows, :].astype(F32) - real).astype(BF16)
                out[1, rows, :] = (rec_ref[1, rows, :].astype(F32) - imag).astype(BF16)


def update(recorded, left, filtered, clip_level):
    block = pl.BlockSpec((2, ROWS, TC), lambda i: (0, 0, jnp.maximum(i - 1, 0)))
    once = dict(pipeline_mode=pl.Buffered(1))
    out = jax.ShapeDtypeStruct((2, ROWS, COLS), BF16)
    blocks = COLS // TC
    return pl.pallas_call(
        update_kernel,
        out_shape=(out, out),
        grid=(blocks + 1,),
        in_specs=[
            block,
            pl.BlockSpec((ROWS, 2 * K), lambda i: (0, 0), **once),
            pl.BlockSpec((NS, 2, 16, TC), lambda i: (0, 0, 0, lax.rem(i + blocks, blocks + 1))),
            pl.BlockSpec((ROWS // 128, 128), lambda i: (0, 0), **once),
        ],
        out_specs=(block, block),
        scratch_shapes=[
            pltpu.VMEM((ROWS, 2 * K), BF16),
            pltpu.VMEM((ROWS, 128), F32),
            pltpu.VMEM((K, TC), BF16),
        ],
        compiler_params=pltpu.CompilerParams(vmem_limit_bytes=60 * 2**20),
        name="update",
    )(recorded, left, filtered, clip_level)


def per_device(recorded, obliquity, clip_level):
    left, filtered = gather(recorded, obliquity)
    return update(recorded, left, filtered, clip_level.reshape(ROWS // 128, 128))


def solution(mesh):
    return jax.shard_map(
        per_device,
        mesh=mesh,
        in_specs=(P(None, "src", "rcv"), P(), P("src")),
        out_specs=(P(None, "src", "rcv"), P(None, "src", "rcv")),
        check_vma=False,
    )
```

time: 54.8 us -> 50.1 us (0.914)
  local copies, waits for them, and re-layouts: 5.15 us -> 0 us
    unnamed x10 -> x0, local copies, waits for them, and re-layouts: 5.15 us -> none
where the time goes in v2:
time: 50.1 us; the launch traced here: 49.9 us
  Pallas kernels  49.2 us (98%)
  between operations  0.64 us (1%)
    pallas_call x1, Pallas kernels, gather(): pl.pallas_call(gather_kernel, out_shape=(jax.ShapeDtypeStruct((ROWS, 2 *...  38.8 us
    pallas_call x1, Pallas kernels, update(): pl.pallas_call(update_kernel, out_shape=(out, out), grid=(blocks + 1,), i...  10.5 us

profile of v2, /device:TPU:1, one launch (start us, length us, event | category | flops | bytes accessed | tf_op | source)
XLA Modules:
  0.0 49.9 jit_solution(11440660360678244923)
XLA Ops:
  0.6 38.8 %gather.1 = (bf16[1024,512]{1,0:T(8,128)(2,1)}, bf16[16,2,16,1280]{3,2,1,0:T(8,128)(2,1)}) custom-call(bf16[2,16,64,1024]{3,2,1,0:T(8,128)(2,1)} %bitcast.2, f32[16,1024]{1,0:T(8,128)} %obl_hbm.1, f32[4,256,256]{2,1,0:T(8,128)} %constant.4.clone.dft_hbm, f32[2,128,128]{2,1,0:T(8,128)} %constant.5.clone.twi_hbm), custom_call_target="tpu_custom_call" | custom-call | tf_op jit(solution)/shard_map/gather/pallas_call | solution.py:335
  39.4 10.5 %update.1 = (bf16[2,1024,1024]{2,1,0:T(8,128)(2,1)}, bf16[2,1024,1024]{2,1,0:T(8,128)(2,1)}) custom-call(bf16[2,1024,1024]{2,1,0:T(8,128)(2,1)} %rec_ref.1, bf16[1024,512]{1,0:T(8,128)(2,1)} %get-tuple-element.4.left_ref, bf16[16,2,16,1280]{3,2,1,0:T(8,128)(2,1)} %get-tuple-element.5.filt_ref, f32[8,128]{1,0:T(8,128)} %bitcast.3), custom_call_target="tpu_custom_call" | custom-call | tf_op jit(solution)/shard_map/update/pallas_call | solution.py:426
